TPU v7x, 128 devices: a whole 4x4x4 slice. The times are simulated.
128 devices in a mesh: pipe: 8 (over x, z_hi), tensor: 16 (over z_lo, y, core).
Axes of the slice: x: 4, y: 4, z: 4 (z_hi: 2, z_lo: 2; z = z_hi * 2 + z_lo), core: 2. Of those that a mesh axis runs over, the one named last changes fastest.
Arguments:
- layer_input: bfloat16 [768, 8192], P('tensor', 'pipe'), may hold values from -6 to 6
- out_grad: bfloat16 [768, 8192], P('tensor', 'pipe'), may hold values from -2 to 2
- gate_pre: bfloat16 [768, 28672], P(None, 'tensor'), may hold values from -8 to 8
- up_pre: bfloat16 [768, 28672], P(None, 'tensor'), may hold values from -6 to 6
- gate_weight: bfloat16 [8192, 28672], P('pipe', 'tensor'), may hold values from -0.0625 to 0.0625
- up_weight: bfloat16 [8192, 28672], P('pipe', 'tensor'), may hold values from -0.0625 to 0.0625
- down_weight: bfloat16 [28672, 8192], P('tensor', 'pipe'), may hold values from -0.03125 to 0.03125
- gate_mask: int32 [64, 224], P('pipe', 'tensor'), may hold values from 0 to 1, as said below
- up_mask: int32 [64, 224], P('pipe', 'tensor'), may hold values from 0 to 1, as said below
- down_mask: int32 [224, 64], P('tensor', 'pipe'), may hold values from 0 to 1, as said below
Outputs:
- grad_input: bfloat16 [768, 8192], P('tensor', 'pipe')
- grad_gate: bfloat16 [8192, 28672], P('pipe', 'tensor')
- grad_up: bfloat16 [8192, 28672], P('pipe', 'tensor')
- grad_down: bfloat16 [28672, 8192], P('tensor', 'pipe')
Inputs may be any that keep to these rules, and one draw needn't show every extreme that they name: `gate_mask`: each entry is 1 for a kept block and 0 for a pruned one; the share of kept blocks differs from block column to block column. `up_mask`: each entry is 1 for a kept block and 0 for a pruned one; the share of kept blocks differs from block column to block column. `down_mask`: each entry is 1 for a kept block and 0 for a pruned one; the share of kept blocks differs from block row to block row.
All inputs are finite; a program needn't handle non-finite values.
Results may differ from a plain program's by a relative error of at most 0.005.
Values may be sent and summed in bfloat16 or wider, within the bound.
A program may use at most 128 MiB of HBM per device.

v0:
```python
import jax
import jax.numpy as jnp
from jax import lax
from jax.sharding import PartitionSpec as P

BLOCK = 128


def expand(mask):
    return jnp.repeat(jnp.repeat(mask, BLOCK, axis=0), BLOCK, axis=1)


def local_grads(hidden_grad, gate_val, up_val, sigma_val):
    gate_grad = (hidden_grad * up_val * sigma_val * (1.0 + gate_val * (1.0 - sigma_val))).astype(
        jnp.bfloat16
    )
    up_grad = (hidden_grad * gate_val * sigma_val).astype(jnp.bfloat16)
    return (gate_grad, up_grad)


def shards(
    layer_input,
    out_grad,
    gate_pre,
    up_pre,
    gate_weight,
    up_weight,
    down_weight,
    gate_mask,
    up_mask,
    down_mask,
):
    mask_gate = expand(gate_mask)
    mask_up = expand(up_mask)
    mask_down = expand(down_mask)
    gate_masked = gate_weight * mask_gate.astype(jnp.bfloat16)
    up_masked = up_weight * mask_up.astype(jnp.bfloat16)
    down_masked = down_weight * mask_down.astype(jnp.bfloat16)
    gate_val = gate_pre.astype(jnp.float32)
    up_val = up_pre.astype(jnp.float32)
    sigma_val = jax.nn.sigmoid(gate_val)
    hidden = (gate_val * sigma_val * up_val).astype(jnp.bfloat16)
    piece = lax.all_gather(out_grad, "tensor", axis=0, tiled=True)
    down_acc = lax.dot_general(
        hidden, piece, (((0,), (0,)), ((), ())), preferred_element_type=jnp.float32
    )
    partial_rows = lax.dot_general(
        piece, down_masked, (((1,), (1,)), ((), ())), preferred_element_type=jnp.float32
    )
    hidden_grad = partial_rows
    down_acc, hidden_partial = (down_acc, hidden_grad)
    grad_down = (down_acc * mask_down.astype(jnp.float32)).astype(jnp.bfloat16)
    hidden_grad = lax.psum(hidden_partial, "pipe")
    gate_grad, up_grad = local_grads(hidden_grad, gate_val, up_val, sigma_val)
    piece = lax.all_gather(layer_input, "tensor", axis=0, tiled=True)
    gate_rows = gate_grad
    up_rows = up_grad
    gate_acc = lax.dot_general(
        piece, gate_rows, (((0,), (0,)), ((), ())), preferred_element_type=jnp.float32
    )
    up_acc = lax.dot_general(
        piece, up_rows, (((0,), (0,)), ((), ())), preferred_element_type=jnp.float32
    )
    gate_acc, up_acc = (gate_acc, up_acc)
    grad_gate = (gate_acc * mask_gate.astype(jnp.float32)).astype(jnp.bfloat16)
    grad_up = (up_acc * mask_up.astype(jnp.float32)).astype(jnp.bfloat16)
    gate_rows = gate_grad
    up_rows = up_grad
    total = lax.dot_general(
        gate_rows, gate_masked, (((1,), (1,)), ((), ())), preferred_element_type=jnp.float32
    )
    grad_input = lax.psum_scatter(
        total
        + lax.dot_general(
            up_rows, up_masked, (((1,), (1,)), ((), ())), preferred_element_type=jnp.float32
        ),
        "tensor",
        scatter_dimension=0,
        tiled=True,
    ).astype(jnp.bfloat16)
    return (grad_input, grad_gate, grad_up, grad_down)


def solution(mesh):
    in_specs = (
        P("tensor", "pipe"),
        P("tensor", "pipe"),
        P(None, "tensor"),
        P(None, "tensor"),
        P("pipe", "tensor"),
        P("pipe", "tensor"),
        P("tensor", "pipe"),
        P("pipe", "tensor"),
        P("pipe", "tensor"),
        P("tensor", "pipe"),
    )
    out_specs = (P("tensor", "pipe"), P("pipe", "tensor"), P("pipe", "tensor"), P("tensor", "pipe"))
    return jax.shard_map(shards, mesh=mesh, in_specs=in_specs, out_specs=out_specs, check_vma=False)
```

profile of v0, /device:TPU:0, one launch (start us, length us, event | category | flops | bytes accessed | tf_op | source)
XLA Modules:
  0.0 404.0 jit_solution(1261620353858778361)
XLA Ops:
  7.9 0.8 fusion.17
  8.8 36.6 %all-gather.3.cloned.1.call-done = bf16[768,1024]{1,0:T(8,128)(2,1)} async-done(((bf16[48,1024]{1,0:T(8,128)(2,1)}), bf16[768,1024]{1,0:T(8,128)(2,1)}) %all-gather.3.cloned.1.call-update) | async-done | bytes 1572880 | tf_op jit(solution)/shard_map/all_gather | solution.py:43
  45.4 5.1 %broadcast_in_dim.31 = bf16[1792,8,128]{2,1,0:T(8,128)(2,1)S(1)} broadcast(bf16[1792,8]{1,0:T(8,128)(2,1)S(1)} %bitcast.66), dimensions={0,1} | broadcast | bytes 3698688 | tf_op jit(solution)/shard_map/broadcast_in_dim | solution.py:10
  50.6 6.4 %convolution_bitcast_fusion = f32[768,1792]{0,1:T(8,128)} fusion(bf16[768,1024]{1,0:T(8,128)(2,1)} %all-gather.3.cloned.1.call-done, bf16[1792,1024]{1,0:T(8,128)(2,1)S(1)} %copy-done.9, bf16[224,8,8,128]{3,2,1,0:T(8,128)(2,1)S(1)} %bitcast.64), kind=kOutput, calls=%fused_computation.22 | convolution fusion | flops 2820407296 | bytes 14417920 | tf_op jit(solution)/shard_map/dot_general | solution.py:47
  58.0 3.3 copy.23
  61.3 4.5 %copy.24 = bf16[768,1792]{0,1:T(8,128)(2,1)} copy(bf16[768,1792]{1,0:T(8,128)(2,1)} %param.12) | data formatting | bytes 5505024 | tf_op args[2]
  66.0 6.0 %copy.26 = bf16[1024,1792]{0,1:T(8,128)(2,1)} copy(bf16[1024,1792]{1,0:T(8,128)(2,1)} %param.14) | data formatting | bytes 7340032 | tf_op args[4]
  72.3 6.0 %copy.28 = bf16[1024,1792]{0,1:T(8,128)(2,1)} copy(bf16[1024,1792]{1,0:T(8,128)(2,1)} %param.15) | data formatting | bytes 7340032 | tf_op args[5]
  78.2 4.3 %bitcast_multiply_fusion.6 = bf16[1024,1792]{0,1:T(8,128)(2,1)} fusion(bf16[1024,1792]{0,1:T(8,128)(2,1)} %copy.26, bf16[1024,14]{0,1:T(8,128)(2,1)S(1)} %bitcast.69), kind=kLoop, calls=%fused_computation.26 | loop fusion | flops 1835008 | bytes 7368704 | tf_op jit(solution)/shard_map/mul | solution.py:36
  82.5 2.1 bitcast_multiply_fusion.5
  84.6 207.2 %all-reduce.2.cloned.1.call-done = f32[768,1792]{0,1:T(8,128)} async-done(((f32[768,1792]{0,1:T(8,128)}), f32[768,1792]{0,1:T(8,128)}) %all-reduce.2.cloned.1.call-update) | async-done | bytes 5505040 | tf_op jit(solution)/shard_map/psum | solution.py:53
  291.8 5.0 %fusion.12 = (bf16[768,1792]{0,1:T(8,128)(2,1)S(1)}, bf16[768,1792]{0,1:T(8,128)(2,1)S(1)}) fusion(f32[768,1792]{0,1:T(8,128)} %all-reduce.2.cloned.1.call-done, bf16[768,1792]{0,1:T(8,128)(2,1)} %copy.24, bf16[768,1792]{0,1:T(8,128)(2,1)S(1)} %copy.23), kind=kLoop, calls=%fused_computation.21 | loop fusion | flops 20643840 | bytes 16515072 | tf_op jit(solution)/shard_map/convert_element_type | solution.py:17
  296.9 3.1 fusion.20
  300.0 0.9 copy-done.1
  300.9 4.9 %convolution_add_fusion = f32[768,1024]{1,0:T(8,128)} fusion(f32[768,1024]{1,0:T(8,128)S(1)} %fusion.20, bf16[768,1792]{0,1:T(8,128)(2,1)S(1)} %get-tuple-element.12, bf16[1024,1792]{0,1:T(8,128)(2,1)S(1)} %copy-done.1), kind=kOutput, calls=%fused_computation.28 | convolution fusion | flops 2819358720 | bytes 12713984 | tf_op jit(solution)/shard_map/dot_general | solution.py:74
  306.4 2.0 broadcast_in_dim.41
  308.7 5.2 %fusion = bf16[1792,1024]{1,0:T(8,128)(2,1)} fusion(f32[224,8,8,128]{3,2,1,0:T(8,128)S(1)} %bitcast.63, bf16[768,1024]{1,0:T(8,128)(2,1)S(1)} %copy-done.10, bf16[768,1792]{0,1:T(8,128)(2,1)S(1)} %copy.23, bf16[768,1792]{0,1:T(8,128)(2,1)S(1)} %copy-done.2), kind=kOutput, calls=%fused_computation.5 | convolution fusion | flops 2833252352 | bytes 18087936 | tf_op jit(solution)/shard_map/dot_general | solution.py:44
  313.9 14.5 %all-gather.5.cloned.1.call-done = bf16[768,1024]{1,0:T(8,128)(2,1)} async-done(((bf16[48,1024]{1,0:T(8,128)(2,1)}), bf16[768,1024]{1,0:T(8,128)(2,1)}) %all-gather.5.cloned.1.call-update) | async-done | bytes 1572880 | tf_op jit(solution)/shard_map/all_gather | solution.py:55
  328.4 7.1 %fusion.2 = bf16[1024,1792]{0,1:T(8,128)(2,1)} fusion(bf16[768,1792]{0,1:T(8,128)(2,1)} %copy-done.6, bf16[768,1024]{1,0:T(8,128)(2,1)} %all-gather.5.cloned.1.call-done, f32[1024,14]{0,1:T(8,128)S(1)} %bitcast.73), kind=kOutput, calls=%fused_computation.9 | convolution fusion | flops 2822242304 | bytes 8052736 | tf_op jit(solution)/shard_map/dot_general | solution.py:58
  335.5 6.1 %copy.32 = bf16[1024,1792]{1,0:T(8,128)(2,1)} copy(bf16[1024,1792]{0,1:T(8,128)(2,1)} %fusion.2) | data formatting | bytes 7340032
  341.6 6.2 %fusion.1 = bf16[1024,1792]{0,1:T(8,128)(2,1)} fusion(bf16[768,1792]{0,1:T(8,128)(2,1)S(1)} %copy-done.4, bf16[768,1024]{1,0:T(8,128)(2,1)} %all-gather.5.cloned.1.call-done, f32[1024,14]{0,1:T(8,128)S(1)} %bitcast.74), kind=kOutput, calls=%fused_computation.7 | convolution fusion | flops 2822242304 | bytes 8052736 | tf_op jit(solution)/shard_map/dot_general | solution.py:61
  347.8 5.9 %copy.33 = bf16[1024,1792]{1,0:T(8,128)(2,1)} copy(bf16[1024,1792]{0,1:T(8,128)(2,1)} %fusion.1) | data formatting | bytes 7340032
  353.7 42.1 %reduce-scatter.2.cloned.1.call-done = f32[48,1024]{1,0:T(8,128)} async-done(((f32[768,1024]{1,0:T(8,128)}), f32[48,1024]{1,0:T(8,128)}) %reduce-scatter.2.cloned.1.call-update) | async-done | bytes 196624 | tf_op jit(solution)/shard_map/reduce_scatter | solution.py:72
  395.9 1.6 convert_element_type.106
  (51 shorter events, 3.0 us)
Async XLA Ops:
  7.2 38.2 %all-gather.3.cloned.1.call-start = ((), (), s32[]{:S(2)}) async-start(), calls=%async_computation.1 | async-start | bytes 1671168 | tf_op jit(solution)/shard_map/all_gather | solution.py:43
  7.9 283.9 %all-reduce.2.cloned.1.call-start = ((), (), s32[]{:S(2)}) async-start(), calls=%async_computation.2 | async-start | bytes 11010048 | tf_op jit(solution)/shard_map/psum | solution.py:53
  45.4 5.2 %copy-start.9 = (bf16[1792,1024]{1,0:T(8,128)(2,1)S(1)}, bf16[1792,1024]{1,0:T(8,128)(2,1)}, u32[]{:S(2)}) copy-start(bf16[1792,1024]{1,0:T(8,128)(2,1)} %param.16) | copy-start | bytes 11010052
  57.0 271.4 %all-gather.5.cloned.1.call-start = ((), (), s32[]{:S(2)}) async-start(), calls=%async_computation.4 | async-start | bytes 1671168 | tf_op jit(solution)/shard_map/all_gather | solution.py:55
  57.7 338.2 %reduce-scatter.2.cloned.1.call-start = ((), (), s32[]{:S(2)}) async-start(), calls=%async_computation.3 | async-start | bytes 3342336 | tf_op jit(solution)/shard_map/reduce_scatter | solution.py:72
  61.3 4.5 %copy-start.7 = (s32[8,14]{1,0:T(8,128)S(1)}, s32[8,14]{1,0:T(8,128)}, u32[]{:S(2)}) copy-start(s32[8,14]{1,0:T(8,128)} %param.17) | copy-start | bytes 1348
  66.0 6.0 %copy-start.8 = (s32[8,14]{1,0:T(8,128)S(1)}, s32[8,14]{1,0:T(8,128)}, u32[]{:S(2)}) copy-start(s32[8,14]{1,0:T(8,128)} %param.18) | copy-start | bytes 1348
  78.2 4.3 %copy-start = (bf16[1024,1792]{0,1:T(8,128)(2,1)S(1)}, bf16[1024,1792]{0,1:T(8,128)(2,1)}, u32[]{:S(2)}) copy-start(bf16[1024,1792]{0,1:T(8,128)(2,1)} %copy.28) | copy-start | bytes 11010052
  291.8 5.1 %copy-start.5 = (bf16[1024,1792]{0,1:T(8,128)(2,1)S(1)}, bf16[1024,1792]{0,1:T(8,128)(2,1)}, u32[]{:S(2)}) copy-start(bf16[1024,1792]{0,1:T(8,128)(2,1)} %bitcast_multiply_fusion.6) | copy-start | bytes 11010052
  296.8 3.1 copy-start.6
  296.9 3.1 copy-start.3
  296.9 4.0 copy-start.1
  306.4 2.1 copy-start.2
  306.4 2.3 copy-start.10
  335.5 6.1 %copy-start.4 = (bf16[768,1792]{0,1:T(8,128)(2,1)S(1)}, bf16[768,1792]{0,1:T(8,128)(2,1)}, u32[]{:S(2)}) copy-start(bf16[768,1792]{0,1:T(8,128)(2,1)} %copy-done.3) | copy-start | bytes 8257540
Sparse Core Ops, SparseCore 0:
  9.7 35.6 all-gather.2
  57.1 234.6 all-reduce.1
  293.5 34.8 all-gather.4
  330.7 65.1 reduce-scatter.1
where the time goes:
time: 405 us; the launch traced here: 404 us
  waiting for transfers between devices  302 us (75%)
  local copies, waits for them, and re-layouts  41.1 us (10%)
  matrix products  32.9 us (8%)
  between operations  14 us (3%)
  other arithmetic  13.7 us (3%)
    psum x1, waiting for transfers between devices, shards(): hidden_grad = lax.psum(hidden_partial, 'pipe')  207 us
    reduce_scatter x1, waiting for transfers between devices, shards(): lax.psum_scatter(total + lax.dot_general(up_rows, up_masked, (((1,), (1,)...  42.1 us
    all_gather x1, waiting for transfers between devices, shards(): piece = lax.all_gather(out_grad, 'tensor', axis=0, tiled=True)  36.6 us
    unnamed x40, local copies, waits for them, and re-layouts  33.3 us
    all_gather x1, waiting for transfers between devices, shards(): piece = lax.all_gather(layer_input, 'tensor', axis=0, tiled=True)  14.5 us
  transfers between devices with their start and end apart: 4, of which 4 were waited for; matrix products, arithmetic and copies ran while one was open for 18% of the time, Pallas kernels for 0%

commit v1 on v0

--- a/solution.py
+++ b/solution.py
@@ -50,7 +50,7 @@
     hidden_grad = partial_rows
     down_acc, hidden_partial = (down_acc, hidden_grad)
     grad_down = (down_acc * mask_down.astype(jnp.float32)).astype(jnp.bfloat16)
-    hidden_grad = lax.psum(hidden_partial, "pipe")
+    hidden_grad = jnp.sum(lax.all_gather(hidden_partial, "pipe"), axis=0)
     gate_grad, up_grad = local_grads(hidden_grad, gate_val, up_val, sigma_val)
     piece = lax.all_gather(layer_input, "tensor", axis=0, tiled=True)
     gate_rows = gate_grad

time: 405 us -> 634 us (1.57)
  waiting for transfers between devices: 302 us -> 477 us
  local copies, waits for them, and re-layouts: 41.1 us -> 77.9 us
  other arithmetic: 13.7 us -> 31.4 us
    all_gather x0 -> x1, waiting for transfers between devices: none -> 409 us  [shards(): hidden_grad = jnp.sum(lax.all_gather(hidden_partial, 'pipe'), axis=0)]
    psum x1 -> x0, waiting for transfers between devices: 207 us -> none  [shards(): hidden_grad = lax.psum(hidden_partial, 'pipe')]
    unnamed x40 -> x41, local copies, waits for them, and re-layouts: 33.3 us -> 69.8 us
    reduce_sum x0 -> x1, other arithmetic: none -> 17.6 us  [shards(): hidden_grad = jnp.sum(lax.all_gather(hidden_partial, 'pipe'), axis=0)]
    all_gather x1, waiting for transfers between devices: 14.5 us -> 0.01 us  [shards(): piece = lax.all_gather(layer_input, 'tensor', axis=0, tiled=True)]
    reduce_scatter x1, waiting for transfers between devices: 42.1 us -> 29.6 us  [shards(): lax.psum_scatter(total + lax.dot_general(up_rows, up_masked, (((1,), (1,)...]
  transfers between devices with their start and end apart: 4 -> 4, of which waited for: 4 -> 3; matrix products, arithmetic and copies ran while one was open for 18% -> 20% of each run, Pallas kernels for 0% -> 0%
where the time goes in v1:
time: 634 us; the launch traced here: 633 us
  waiting for transfers between devices  477 us (75%)
  local copies, waits for them, and re-layouts  77.9 us (12%)
  matrix products  32.9 us (5%)
  other arithmetic  31.4 us (5%)
  between operations  14 us (2%)
    all_gather x1, waiting for transfers between devices, shards(): hidden_grad = jnp.sum(lax.all_gather(hidden_partial, 'pipe'), axis=0)  409 us
    unnamed x41, local copies, waits for them, and re-layouts  69.8 us
    all_gather x1, waiting for transfers between devices, shards(): piece = lax.all_gather(out_grad, 'tensor', axis=0, tiled=True)  36.6 us
    reduce_scatter x1, waiting for transfers between devices, shards(): lax.psum_scatter(total + lax.dot_general(up_rows, up_masked, (((1,), (1,)...  29.6 us
    reduce_sum x1, other arithmetic, shards(): hidden_grad = jnp.sum(lax.all_gather(hidden_partial, 'pipe'), axis=0)  17.6 us
  transfers between devices with their start and end apart: 4, of which 3 were waited for; matrix products, arithmetic and copies ran while one was open for 20% of the time, Pallas kernels for 0%

profile of v1, /device:TPU:0, one launch (start us, length us, event | category | flops | bytes accessed | tf_op | source)
XLA Modules:
  0.0 633.0 jit_solution(15458881887943194331)
XLA Ops:
  8.8 36.6 %all-gather.5.cloned.1.call-done = bf16[768,1024]{1,0:T(8,128)(2,1)} async-done(((bf16[48,1024]{1,0:T(8,128)(2,1)}), bf16[768,1024]{1,0:T(8,128)(2,1)}) %all-gather.5.cloned.1.call-update) | async-done | bytes 1572880 | tf_op jit(solution)/shard_map/all_gather | solution.py:43
  45.4 5.1 broadcast_in_dim.31
  50.6 6.3 convolution_bitcast_fusion
  57.8 3.3 copy.31
  61.2 4.5 copy.32
  65.9 6.5 %copy.34 = bf16[1024,1792]{0,1:T(8,128)(2,1)} copy(bf16[1024,1792]{1,0:T(8,128)(2,1)} %param.14) | data formatting | bytes 7340032 | tf_op args[4]
  72.7 6.1 copy.36
  78.8 4.3 bitcast_multiply_fusion.6
  83.1 2.1 bitcast_multiply_fusion.5
  85.2 409.1 %all-gather.9.cloned.1.call-done = f32[6144,1792]{0,1:T(8,128)} async-done(((f32[768,1792]{0,1:T(8,128)}), f32[6144,1792]{0,1:T(8,128)}) %all-gather.9.cloned.1.call-update) | async-done | bytes 44040208 | tf_op jit(solution)/shard_map/all_gather | solution.py:53
  494.2 36.0 %copy.43 = f32[224,8,8,768]{3,2,1,0:T(8,128)} copy(f32[224,8,8,768]{3,1,2,0:T(8,128)} %bitcast.68) | data formatting | bytes 88080384
  530.3 17.6 %bitcast_reduce_fusion = f32[768,1792]{0,1:T(8,128)} fusion(f32[224,8,8,768]{3,2,1,0:T(8,128)} %copy.43), kind=kLoop, calls=%fused_computation | loop fusion | flops 9633792 | bytes 49545216 | tf_op jit(solution)/shard_map/reduce_sum | solution.py:53
  547.9 5.0 fusion.12
  553.0 3.1 fusion.20
  556.1 0.9 copy-done.1
  557.0 4.9 convolution_add_fusion
  562.5 2.3 broadcast_in_dim.41
  564.8 5.2 fusion
  570.0 7.1 %fusion.2 = bf16[1024,1792]{0,1:T(8,128)(2,1)} fusion(bf16[768,1792]{0,1:T(8,128)(2,1)} %copy-done.6, bf16[768,1024]{1,0:T(8,128)(2,1)} %all-gather.7.cloned.1.call-done, f32[1024,14]{0,1:T(8,128)S(1)} %bitcast.79), kind=kOutput, calls=%fused_computation.10 | convolution fusion | flops 2822242304 | bytes 8052736 | tf_op jit(solution)/shard_map/dot_general | solution.py:58
  577.1 6.1 copy.40
  583.2 6.2 fusion.1
  589.4 5.9 copy.41
  595.3 29.6 %reduce-scatter.2.cloned.1.call-done = f32[48,1024]{1,0:T(8,128)} async-done(((f32[768,1024]{1,0:T(8,128)}), f32[48,1024]{1,0:T(8,128)}) %reduce-scatter.2.cloned.1.call-update) | async-done | bytes 196624 | tf_op jit(solution)/shard_map/reduce_scatter | solution.py:72
  624.9 1.6 convert_element_type.106
  (53 shorter events, 3.6 us)
Async XLA Ops:
  7.2 38.2 %all-gather.5.cloned.1.call-start = ((), (), s32[]{:S(2)}) async-start(), calls=%async_computation.1 | async-start | bytes 1671168 | tf_op jit(solution)/shard_map/all_gather | solution.py:43
  7.9 486.3 %all-gather.9.cloned.1.call-start = ((), (), s32[]{:S(2)}) async-start(), calls=%async_computation.4 | async-start | bytes 49545216 | tf_op jit(solution)/shard_map/all_gather | solution.py:53
  45.4 5.2 copy-start.9
  56.9 513.1 %all-gather.7.cloned.1.call-start = ((), (), s32[]{:S(2)}) async-start(), calls=%async_computation.3 | async-start | bytes 1671168 | tf_op jit(solution)/shard_map/all_gather | solution.py:55
  57.6 567.3 %reduce-scatter.2.cloned.1.call-start = ((), (), s32[]{:S(2)}) async-start(), calls=%async_computation.2 | async-start | bytes 3342336 | tf_op jit(solution)/shard_map/reduce_scatter | solution.py:72
  61.2 4.5 copy-start.7
  65.9 6.5 %copy-start.8 = (s32[8,14]{1,0:T(8,128)S(1)}, s32[8,14]{1,0:T(8,128)}, u32[]{:S(2)}) copy-start(s32[8,14]{1,0:T(8,128)} %param.18) | copy-start | bytes 1348
  78.8 4.3 copy-start
  547.9 5.1 copy-start.5
  552.9 3.1 copy-start.6
  552.9 3.1 copy-start.3
  553.0 4.0 copy-start.1
  562.5 2.3 copy-start.2
  562.5 2.3 copy-start.10
  577.1 6.1 copy-start.4
Sparse Core Ops, SparseCore 0:
  9.7 35.6 all-gather.4
  57.0 437.1 all-gather.8
  495.9 30.8 all-gather.6
  562.1 62.8 reduce-scatter.1
